TPU v7x, 128 devices: a whole 4x4x4 slice. The times are simulated.
128 devices in a mesh: leaf: 4 (over y), rows: 32 (over z, x, core).
Axes of the slice: x: 4, y: 4, z: 4, core: 2. Of those that a mesh axis runs over, the one named last changes fastest.
Arguments:
- leaf_rhs: float32 [8, 16, 2048], P(None, 'leaf', 'rows'), may hold values from -6 to 6
- parent_rhs: float32 [8, 4, 4096], P(None, 'leaf', 'rows'), may hold values from -6 to 6
- root_rhs: float32 [8, 4096], P(None, ('leaf', 'rows')), may hold values from -6 to 6
- leaf_inv: bfloat16 [16, 2048, 2048], P('leaf', 'rows'), as said below
- leaf_panel: bfloat16 [16, 8192, 2048], P('leaf', 'rows'), may hold values from -0.0625 to 0.0625
- leaf_rows: int32 [16, 8192], P('leaf', 'rows'), may hold values from 0 to 8191, as said below
- leaf_height: int32 [16], P('leaf'), may hold values from 2048 to 8192
- parent_inv: bfloat16 [4, 4096, 4096], P('leaf', 'rows'), as said below
- parent_panel: bfloat16 [4, 4096, 4096], P('leaf', 'rows'), may hold values from -0.046875 to 0.046875
- parent_rows: int32 [4, 4096], P('leaf', 'rows'), may hold values from 0 to 4095, as said below
- parent_height: int32 [4], P('leaf'), may hold values from 1024 to 4096
- root_inv: bfloat16 [4096, 4096], P('rows'), as said below
Outputs:
- leaf_solution: float32 [8, 16, 2048], P(None, 'leaf', 'rows')
- parent_solution: float32 [8, 4, 4096], P(None, 'leaf', 'rows')
- root_solution: float32 [8, 4096], P(None, ('leaf', 'rows'))
Inputs may be any that keep to these rules, and one draw needn't show every extreme that they name: `leaf_rows`: each leaf's first leaf_height entries are distinct and ascending; every entry is a valid ancestor index. `parent_rows`: each parent's first parent_height entries are distinct and ascending. `leaf_inv`: A dense well conditioned matrix. `parent_inv`: A dense well conditioned matrix. `root_inv`: A dense well conditioned matrix.
All inputs are finite; a program needn't handle non-finite values.
Results may differ from a plain program's by a relative error of at most 0.009.
Values may be sent and summed in bfloat16 or wider, within the bound.
A program may use at most 64 MiB of HBM per device.

v0:
```python
import jax
import jax.numpy as jnp
from jax import lax
from jax.sharding import PartitionSpec as P


def shards(
    leaf_rhs,
    parent_rhs,
    root_rhs,
    leaf_inv,
    leaf_panel,
    leaf_rows,
    leaf_height,
    parent_inv,
    parent_panel,
    parent_rows,
    parent_height,
    root_inv,
):
    rcount = leaf_rhs.shape[0]
    group_leaves = leaf_rhs.shape[1]
    leaf_local = leaf_panel.shape[1]
    parent_width = parent_inv.shape[2]
    root_width = root_inv.shape[1]
    row_index = lax.axis_index("rows")
    parent_cols = parent_rhs.shape[2]
    root_cols = root_rhs.shape[1]
    flat_index = lax.axis_index("leaf") * lax.axis_size("rows") + row_index
    block = leaf_inv
    ly = jnp.einsum(
        "rln,lin->rli",
        lax.all_gather(leaf_rhs.astype(jnp.bfloat16), "rows", axis=2, tiled=True),
        block,
        preferred_element_type=jnp.float32,
    )
    lyb = ly.astype(jnp.bfloat16)
    block = leaf_panel
    lupd = jnp.einsum(
        "rln,lhn->rlh",
        lax.all_gather(lyb, "rows", axis=2, tiled=True),
        block,
        preferred_element_type=jnp.float32,
    )
    leaf_pos = row_index * leaf_local + jnp.arange(leaf_local, dtype=jnp.int32)
    leaf_mask = leaf_pos[None, :] < leaf_height[:, None]
    lupd = jnp.where(leaf_mask[None, :, :], lupd, 0.0)
    leaf_flat = leaf_rows.reshape(-1)
    local_acc = (
        jnp.zeros((rcount, parent_width + root_width), jnp.float32)
        .at[:, leaf_flat]
        .add(lupd.reshape(rcount, -1))
    )
    group_acc = lax.psum(local_acc, "rows")
    parent_acc = group_acc[:, :parent_width]
    root_from_leaves = lax.psum(group_acc[:, parent_width:], "leaf")
    parent_slice = lax.dynamic_slice_in_dim(parent_acc, row_index * parent_cols, parent_cols, 1)
    prb = (parent_rhs[:, 0, :] - parent_slice).astype(jnp.bfloat16)
    inverse_rows = parent_inv[0]
    panel_rows = parent_panel[0]
    block = inverse_rows
    py = jnp.dot(
        lax.all_gather(prb, "rows", axis=1, tiled=True), block.T, preferred_element_type=jnp.float32
    )
    pyb = py.astype(jnp.bfloat16)
    parent_local = panel_rows.shape[0]
    block = panel_rows
    pupd = jnp.dot(
        lax.all_gather(pyb, "rows", axis=1, tiled=True), block.T, preferred_element_type=jnp.float32
    )
    parent_pos = row_index * parent_local + jnp.arange(parent_local, dtype=jnp.int32)
    parent_mask = parent_pos < parent_height[0]
    pupd = jnp.where(parent_mask[None, :], pupd, 0.0)
    parent_root = jnp.zeros((rcount, root_width), jnp.float32).at[:, parent_rows[0]].add(pupd)
    root_acc = root_from_leaves + lax.psum(parent_root, ("leaf", "rows"))
    root_slice = lax.dynamic_slice_in_dim(root_acc, flat_index * root_cols, root_cols, 1)
    rrb = (root_rhs - root_slice).astype(jnp.bfloat16)
    block = root_inv
    ry = jnp.dot(
        lax.all_gather(rrb, ("leaf", "rows"), axis=1, tiled=True),
        block.T,
        preferred_element_type=jnp.float32,
    )
    root_term = jnp.dot(ry.astype(jnp.bfloat16), root_inv, preferred_element_type=jnp.float32)
    root_full = lax.psum(root_term, "rows")
    root_solution = lax.dynamic_slice_in_dim(root_full, flat_index * root_cols, root_cols, 1)
    rxb = root_full.astype(jnp.bfloat16)
    parent_anc = rxb[:, parent_rows[0]]
    parent_anc = jnp.where(parent_mask[None, :], parent_anc, jnp.zeros_like(parent_anc))
    parent_term = jnp.dot(parent_anc, panel_rows, preferred_element_type=jnp.float32)
    parent_tail = lax.psum_scatter(parent_term, "rows", scatter_dimension=1, tiled=True)
    pvb = (py - parent_tail).astype(jnp.bfloat16)
    parent_sol_term = jnp.dot(pvb, inverse_rows, preferred_element_type=jnp.float32)
    parent_sol = lax.psum_scatter(parent_sol_term, "rows", scatter_dimension=1, tiled=True)
    parent_whole = lax.all_gather(parent_sol.astype(jnp.bfloat16), "rows", axis=1, tiled=True)
    ancestors = jnp.concatenate([parent_whole, rxb], axis=1)
    leaf_anc = ancestors[:, leaf_flat].reshape(rcount, group_leaves, leaf_local)
    leaf_anc = jnp.where(leaf_mask[None, :, :], leaf_anc, jnp.zeros_like(leaf_anc))
    leaf_term = jnp.einsum("rlh,lhc->rlc", leaf_anc, leaf_panel, preferred_element_type=jnp.float32)
    leaf_tail = lax.psum_scatter(leaf_term, "rows", scatter_dimension=2, tiled=True)
    lvb = (ly - leaf_tail).astype(jnp.bfloat16)
    leaf_sol_term = jnp.einsum("rli,lic->rlc", lvb, leaf_inv, preferred_element_type=jnp.float32)
    leaf_sol = lax.psum_scatter(leaf_sol_term, "rows", scatter_dimension=2, tiled=True)
    return (leaf_sol, parent_sol[:, None, :], root_solution)


def solution(mesh):
    return jax.shard_map(
        shards,
        mesh=mesh,
        in_specs=(
            P(None, "leaf", "rows"),
            P(None, "leaf", "rows"),
            P(None, ("leaf", "rows")),
            P("leaf", "rows", None),
            P("leaf", "rows", None),
            P("leaf", "rows"),
            P("leaf"),
            P("leaf", "rows", None),
            P("leaf", "rows", None),
            P("leaf", "rows"),
            P("leaf"),
            P("rows", None),
        ),
        out_specs=(P(None, "leaf", "rows"), P(None, "leaf", "rows"), P(None, ("leaf", "rows"))),
        check_vma=False,
    )
```

profile of v0, /device:TPU:0, one launch (start us, length us, event | category | flops | bytes accessed | tf_op | source)
XLA Modules:
  0.0 916.0 jit_solution(10626270217796478974)
XLA Ops:
  7.2 0.8 copy.81
  8.0 0.7 copy.91
  8.9 27.5 %all_gather.18 = bf16[8,4,2048]{0,1,2:T(4,128)(2,1)S(1)} all-gather(bf16[8,4,64]{0,1,2:T(4,128)(2,1)S(1)} %copy.62), channel_id=1, replica_groups=mesh['leaf'=4,'rows'=32] {'rows'}, dimensions={2}, use_global_device_ids=true | all-gather | bytes 135168 | tf_op jit(solution)/shard_map/all_gather | solution.py:33
  36.4 0.8 fusion.36
  37.3 25.3 %all_gather.19 = bf16[8,4,2048]{0,1,2:T(4,128)(2,1)S(1)} all-gather(bf16[8,4,64]{0,1,2:T(4,128)(2,1)S(1)} %copy.64), channel_id=1, replica_groups=mesh['leaf'=4,'rows'=32] {'rows'}, dimensions={2}, use_global_device_ids=true | all-gather | bytes 135168 | tf_op jit(solution)/shard_map/all_gather | solution.py:41
  62.7 3.4 fusion.6
  66.1 0.2 copy.66
  66.3 8.2 scatter_custom_fusion
  74.5 3.5 copy.67
  78.9 100.7 %all-reduce.5.cloned.1.call-done = f32[8,8192]{1,0:T(8,128)} async-done(((f32[8,8192]{1,0:T(8,128)}), f32[8,8192]{1,0:T(8,128)}) %all-reduce.5.cloned.1.call-update) | async-done | bytes 262160 | tf_op jit(solution)/shard_map/psum | solution.py:54
  179.6 1.6 fusion.35
  181.2 24.6 %all_gather.20 = bf16[8,4096]{1,0:T(8,128)(2,1)S(1)} all-gather(bf16[8,128]{1,0:T(8,128)(2,1)S(1)} %subtract_convert_fusion.3), channel_id=1, replica_groups=mesh['leaf'=4,'rows'=32] {'rows'}, dimensions={1}, use_global_device_ids=true | all-gather | bytes 67584 | tf_op jit(solution)/shard_map/all_gather | solution.py:63
  205.9 0.4 fusion.37
  206.2 21.5 %all_gather.21 = bf16[8,4096]{1,0:T(8,128)(2,1)S(1)} all-gather(bf16[8,128]{1,0:T(8,128)(2,1)S(1)} %get-tuple-element.22), channel_id=1, replica_groups=mesh['leaf'=4,'rows'=32] {'rows'}, dimensions={1}, use_global_device_ids=true | all-gather | bytes 67584 | tf_op jit(solution)/shard_map/all_gather | solution.py:69
  227.8 0.4 fusion.12
  228.3 1.5 scatter_custom_fusion.1
  229.8 1.2 copy.69
  231.1 0.7 all-reduce.7.cloned.1.call-update
  231.8 141.0 %all-reduce.9.cloned.1.call-done = f32[8,4096]{1,0:T(8,128)} async-done(((f32[8,4096]{1,0:T(8,128)}), f32[8,4096]{1,0:T(8,128)}) %all-reduce.9.cloned.1.call-update) | async-done | bytes 131088 | tf_op jit(solution)/shard_map/psum | solution.py:75
  372.8 41.1 %all-reduce.7.cloned.1.call-done = f32[8,4096]{1,0:T(8,128)} async-done(((f32[8,4096]{1,0:T(8,128)}), f32[8,4096]{1,0:T(8,128)}) %all-reduce.7.cloned.1.call-update) | async-done | bytes 131088 | tf_op jit(solution)/shard_map/psum | solution.py:56
  413.9 0.8 fusion.31
  414.7 35.9 %all-gather = bf16[128,32,8]{1,2,0:T(8,128)(2,1)S(1)} all-gather(bf16[1,32,8]{1,2,0:T(8,128)(2,1)S(1)} %fusion.31), channel_id=1, replica_groups=mesh['leaf'=4,'rows'=32] {'leaf','rows'}, dimensions={0}, use_global_device_ids=true | all-gather | bytes 66048 | tf_op jit(solution)/shard_map/all_gather | solution.py:80
  450.6 0.3 reshape.142
  450.9 3.2 fusion.13
  454.2 98.7 %all-reduce.11.cloned.1.call-done = f32[8,4096]{1,0:T(8,128)} async-done(((f32[8,4096]{1,0:T(8,128)}), f32[8,4096]{1,0:T(8,128)}) %all-reduce.11.cloned.1.call-update) | async-done | bytes 131088 | tf_op jit(solution)/shard_map/psum | solution.py:85
  552.9 0.9 convert_element_type.36
  553.8 1.3 copy.71
  555.1 2.0 gather_fusion
  557.1 1.0 fusion.14
  558.2 71.9 %reduce-scatter.9.cloned.1.call-done = f32[8,128]{1,0:T(8,128)} async-done(((f32[8,4096]{1,0:T(8,128)}), f32[8,128]{1,0:T(8,128)}) %reduce-scatter.9.cloned.1.call-update) | async-done | bytes 4112 | tf_op jit(solution)/shard_map/reduce_scatter | solution.py:91
  630.1 1.6 fusion.17
  631.7 73.8 %reduce-scatter.11.cloned.1.call-done = f32[8,128]{1,0:T(8,128)} async-done(((f32[8,4096]{1,0:T(8,128)}), f32[8,128]{1,0:T(8,128)}) %reduce-scatter.11.cloned.1.call-update) | async-done | bytes 4112 | tf_op jit(solution)/shard_map/reduce_scatter | solution.py:94
  705.5 0.7 convert_element_type.38
  706.2 23.5 %all_gather.23 = bf16[8,4096]{1,0:T(8,128)(2,1)S(1)} all-gather(bf16[8,128]{1,0:T(8,128)(2,1)S(1)} %convert_element_type.38), channel_id=1, replica_groups=mesh['leaf'=4,'rows'=32] {'rows'}, dimensions={1}, use_global_device_ids=true | all-gather | bytes 67584 | tf_op jit(solution)/shard_map/all_gather | solution.py:95
  729.7 1.0 copy.72
  730.7 3.2 gather_fusion.1
  734.1 2.8 convolution_bitcast_fusion.1
  736.9 3.1 copy.76
  740.0 4.5 reshape.143
  744.6 76.7 %reduce-scatter.13.cloned.1.call-done = f32[64,32]{1,0:T(8,128)} async-done(((f32[2048,32]{1,0:T(8,128)}), f32[64,32]{1,0:T(8,128)}) %reduce-scatter.13.cloned.1.call-update) | async-done | bytes 8208
  821.3 0.9 reshape.144
  822.3 0.3 convolution_bitcast_fusion
  822.6 3.1 copy.78
  825.6 4.5 reshape.145
  830.2 1.3 constant_dynamic-slice_fusion
  831.6 76.0 %reduce-scatter.15.cloned.1.call-done = f32[64,32]{1,0:T(8,128)} async-done(((f32[2048,32]{1,0:T(8,128)}), f32[64,32]{1,0:T(8,128)}) %reduce-scatter.15.cloned.1.call-update) | async-done | bytes 8208
  907.6 0.9 reshape.146
  908.5 0.7 copy.74
  (48 shorter events, 1.2 us)
Async XLA Ops:
  7.2 29.2 %copy-start = (bf16[4,64,2048]{2,1,0:T(8,128)(2,1)S(1)}, bf16[4,64,2048]{2,1,0:T(8,128)(2,1)}, u32[]{:S(2)}) copy-start(bf16[4,64,2048]{2,1,0:T(8,128)(2,1)} %param.15) | copy-start | bytes 3145732
  7.2 172.4 %all-reduce.5.cloned.1.call-start = ((), (), s32[]{:S(2)}) async-start(), calls=%async_computation.4 | async-start | bytes 524288 | tf_op jit(solution)/shard_map/psum | solution.py:54
  36.3 26.3 %copy-start.7 = (s32[4]{0:T(128)S(1)}, s32[4]{0:T(128)}, u32[]{:S(2)}) copy-start(s32[4]{0:T(128)} %param.18) | copy-start | bytes 52
  74.5 3.6 copy-start.8
  74.5 106.7 %copy-start.5 = (f32[8,1,128]{2,1,0:T(1,128)S(1)}, f32[8,1,128]{2,1,0:T(1,128)}, u32[]{:S(2)}) copy-start(f32[8,1,128]{2,1,0:T(1,128)} %param.13) | copy-start | bytes 12292
  74.5 131.4 %copy-start.3 = (bf16[1,128,4096]{2,1,0:T(8,128)(2,1)S(1)}, bf16[1,128,4096]{2,1,0:T(8,128)(2,1)}, u32[]{:S(2)}) copy-start(bf16[1,128,4096]{2,1,0:T(8,128)(2,1)} %param.19) | copy-start | bytes 3145732
  78.0 149.7 %copy-start.1 = (bf16[1,128,4096]{2,1,0:T(8,128)(2,1)S(1)}, bf16[1,128,4096]{2,1,0:T(8,128)(2,1)}, u32[]{:S(2)}) copy-start(bf16[1,128,4096]{2,1,0:T(8,128)(2,1)} %param.20) | copy-start | bytes 3145732
  78.1 294.8 %all-reduce.9.cloned.1.call-start = ((), (), s32[]{:S(2)}) async-start(), calls=%async_computation.6 | async-start | bytes 262144 | tf_op jit(solution)/shard_map/psum | solution.py:75
  228.2 185.7 %copy-start.6 = (f32[8,32]{1,0:T(8,128)S(1)}, f32[8,32]{1,0:T(8,128)}, u32[]{:S(2)}) copy-start(f32[8,32]{1,0:T(8,128)} %param.14) | copy-start | bytes 3076
  231.0 182.9 %all-reduce.7.cloned.1.call-start = ((), (), s32[]{:S(2)}) async-start(), calls=%async_computation.5 | async-start | bytes 262144 | tf_op jit(solution)/shard_map/psum | solution.py:56
  231.8 321.1 %all-reduce.11.cloned.1.call-start = ((), (), s32[]{:S(2)}) async-start(), calls=%async_computation.7 | async-start | bytes 262144 | tf_op jit(solution)/shard_map/psum | solution.py:85
  450.6 106.5 %copy-start.2 = (bf16[1,128,4096]{2,1,0:T(8,128)(2,1)S(1)}, bf16[1,128,4096]{2,1,0:T(8,128)(2,1)}, u32[]{:S(2)}) copy-start(bf16[1,128,4096]{2,1,0:T(8,128)(2,1)} %param.20) | copy-start | bytes 3145732
  450.9 179.2 %copy-start.4 = (bf16[1,128,4096]{2,1,0:T(8,128)(2,1)S(1)}, bf16[1,128,4096]{2,1,0:T(8,128)(2,1)}, u32[]{:S(2)}) copy-start(bf16[1,128,4096]{2,1,0:T(8,128)(2,1)} %param.19) | copy-start | bytes 3145732
  454.1 176.0 %reduce-scatter.9.cloned.1.call-start = ((), (), s32[]{:S(2)}) async-start(), calls=%async_computation.8 | async-start | bytes 135168 | tf_op jit(solution)/shard_map/reduce_scatter | solution.py:91
  558.1 147.3 %reduce-scatter.11.cloned.1.call-start = ((), (), s32[]{:S(2)}) async-start(), calls=%async_computation.9 | async-start | bytes 135168 | tf_op jit(solution)/shard_map/reduce_scatter | solution.py:94
  631.7 189.7 %reduce-scatter.13.cloned.1.call-start = ((), (), s32[]{:S(2)}) async-start(), calls=%async_computation.10 | async-start | bytes 1081344
  744.6 163.0 %reduce-scatter.15.cloned.1.call-start = ((), (), s32[]{:S(2)}) async-start(), calls=%async_computation.11 | async-start | bytes 1081344
Sparse Core Ops, SparseCore 0:
  78.2 101.3 all-reduce.4
  231.2 141.6 all-reduce.8
  375.1 38.7 all-reduce.6
  454.2 98.5 all-reduce.10
  558.3 71.7 reduce-scatter.8
  633.9 71.5 reduce-scatter.10
  744.7 76.6 reduce-scatter.12
  830.3 77.2 reduce-scatter.14
where the time goes:
time: 917 us; the launch traced here: 916 us
  waiting for transfers between devices  681 us (74%)
  blocking collectives  158 us (17%)
  local copies, waits for them, and re-layouts  35.6 us (4%)
  between operations  15 us (2%)
  matrix products  13.8 us (2%)
  other arithmetic  12.2 us (1%)
    unnamed x10, waiting for transfers between devices  154 us
    psum x1, waiting for transfers between devices, shards(): root_acc = root_from_leaves + lax.psum(parent_root, ('leaf', 'rows'))  141 us
    psum x1, waiting for transfers between devices, shards(): group_acc = lax.psum(local_acc, 'rows')  101 us
    psum x1, waiting for transfers between devices, shards(): root_full = lax.psum(root_term, 'rows')  98.7 us
    reduce_scatter x1, waiting for transfers between devices, shards(): lax.psum_scatter(parent_sol_term, 'rows', scatter_dimension=1, tiled=True)  73.8 us
    reduce_scatter x1, waiting for transfers between devices, shards(): lax.psum_scatter(parent_term, 'rows', scatter_dimension=1, tiled=True)  71.9 us
    psum x1, waiting for transfers between devices, shards(): root_from_leaves = lax.psum(group_acc[:, parent_width:], 'leaf')  41.1 us
    all_gather x1, blocking collectives, shards(): lax.all_gather(rrb, ('leaf', 'rows'), axis=1, tiled=True)  35.9 us
  transfers between devices with their start and end apart: 8, of which 8 were waited for; matrix products, arithmetic and copies ran while one was open for 0% of the time, Pallas kernels for 0%

commit v1 on v0

--- a/solution.py
+++ b/solution.py
@@ -2,6 +2,7 @@
 import jax.numpy as jnp
 from jax import lax
 from jax.sharding import PartitionSpec as P
+from jax.lax import all_gather
 
 
 def shards(
@@ -82,7 +83,7 @@
         preferred_element_type=jnp.float32,
     )
     root_term = jnp.dot(ry.astype(jnp.bfloat16), root_inv, preferred_element_type=jnp.float32)
-    root_full = lax.psum(root_term, "rows")
+    root_full = all_gather(root_term, axis_name="rows").sum(axis=0)
     root_solution = lax.dynamic_slice_in_dim(root_full, flat_index * root_cols, root_cols, 1)
     rxb = root_full.astype(jnp.bfloat16)
     parent_anc = rxb[:, parent_rows[0]]

time: 917 us -> 865 us (0.943)
  waiting for transfers between devices: 681 us -> 626 us
    psum x1 -> x0, waiting for transfers between devices: 98.7 us -> none  [shards(): root_full = lax.psum(root_term, 'rows')]
    all_gather x0 -> x1, waiting for transfers between devices: none -> 43.7 us  [shards(): root_full = all_gather(root_term, axis_name='rows').sum(axis=0)]
where the time goes in v1:
time: 865 us; the launch traced here: 864 us
  waiting for transfers between devices  626 us (72%)
  blocking collectives  158 us (18%)
  local copies, waits for them, and re-layouts  37 us (4%)
  between operations  15 us (2%)
  matrix products  13.8 us (2%)
  other arithmetic  13.7 us (2%)
    unnamed x10, waiting for transfers between devices  154 us
    psum x1, waiting for transfers between devices, shards(): root_acc = root_from_leaves + lax.psum(parent_root, ('leaf', 'rows'))  141 us
    psum x1, waiting for transfers between devices, shards(): group_acc = lax.psum(local_acc, 'rows')  101 us
    reduce_scatter x1, waiting for transfers between devices, shards(): lax.psum_scatter(parent_sol_term, 'rows', scatter_dimension=1, tiled=True)  73.8 us
    reduce_scatter x1, waiting for transfers between devices, shards(): lax.psum_scatter(parent_term, 'rows', scatter_dimension=1, tiled=True)  71.7 us
    all_gather x1, waiting for transfers between devices, shards(): root_full = all_gather(root_term, axis_name='rows').sum(axis=0)  43.7 us
    psum x1, waiting for transfers between devices, shards(): root_from_leaves = lax.psum(group_acc[:, parent_width:], 'leaf')  41.1 us
    all_gather x1, blocking collectives, shards(): lax.all_gather(rrb, ('leaf', 'rows'), axis=1, tiled=True)  35.9 us
  transfers between devices with their start and end apart: 8, of which 8 were waited for; matrix products, arithmetic and copies ran while one was open for 0% of the time, Pallas kernels for 0%

profile of v1, /device:TPU:0, one launch (start us, length us, event | category | flops | bytes accessed | tf_op | source)
XLA Modules:
  0.0 864.3 jit_solution(8437186229718488752)
XLA Ops:
  7.2 0.8 copy.81
  8.0 0.7 copy.91
  8.9 27.5 %all_gather.24 = bf16[8,4,2048]{0,1,2:T(4,128)(2,1)S(1)} all-gather(bf16[8,4,64]{0,1,2:T(4,128)(2,1)S(1)} %copy.62), channel_id=1, replica_groups=mesh['leaf'=4,'rows'=32] {'rows'}, dimensions={2}, use_global_device_ids=true | all-gather | bytes 135168 | tf_op jit(solution)/shard_map/all_gather | solution.py:34
  36.4 0.8 fusion.36
  37.3 25.3 %all_gather.25 = bf16[8,4,2048]{0,1,2:T(4,128)(2,1)S(1)} all-gather(bf16[8,4,64]{0,1,2:T(4,128)(2,1)S(1)} %copy.64), channel_id=1, replica_groups=mesh['leaf'=4,'rows'=32] {'rows'}, dimensions={2}, use_global_device_ids=true | all-gather | bytes 135168 | tf_op jit(solution)/shard_map/all_gather | solution.py:42
  62.7 3.4 fusion.6
  66.3 8.2 scatter_custom_fusion
  74.5 3.5 copy.67
  78.9 100.7 %all-reduce.4.cloned.1.call-done = f32[8,8192]{1,0:T(8,128)} async-done(((f32[8,8192]{1,0:T(8,128)}), f32[8,8192]{1,0:T(8,128)}) %all-reduce.4.cloned.1.call-update) | async-done | bytes 262160 | tf_op jit(solution)/shard_map/psum | solution.py:55
  179.6 1.6 fusion.35
  181.2 24.6 %all_gather.26 = bf16[8,4096]{1,0:T(8,128)(2,1)S(1)} all-gather(bf16[8,128]{1,0:T(8,128)(2,1)S(1)} %subtract_convert_fusion.3), channel_id=1, replica_groups=mesh['leaf'=4,'rows'=32] {'rows'}, dimensions={1}, use_global_device_ids=true | all-gather | bytes 67584 | tf_op jit(solution)/shard_map/all_gather | solution.py:64
  205.9 0.4 fusion.37
  206.2 21.5 %all_gather.27 = bf16[8,4096]{1,0:T(8,128)(2,1)S(1)} all-gather(bf16[8,128]{1,0:T(8,128)(2,1)S(1)} %get-tuple-element.22), channel_id=1, replica_groups=mesh['leaf'=4,'rows'=32] {'rows'}, dimensions={1}, use_global_device_ids=true | all-gather | bytes 67584 | tf_op jit(solution)/shard_map/all_gather | solution.py:70
  227.8 0.4 fusion.12
  228.3 1.5 scatter_custom_fusion.1
  229.8 1.2 copy.69
  231.1 0.7 all-reduce.6.cloned.1.call-update
  231.8 141.0 %all-reduce.8.cloned.1.call-done = f32[8,4096]{1,0:T(8,128)} async-done(((f32[8,4096]{1,0:T(8,128)}), f32[8,4096]{1,0:T(8,128)}) %all-reduce.8.cloned.1.call-update) | async-done | bytes 131088 | tf_op jit(solution)/shard_map/psum | solution.py:76
  372.8 41.1 %all-reduce.6.cloned.1.call-done = f32[8,4096]{1,0:T(8,128)} async-done(((f32[8,4096]{1,0:T(8,128)}), f32[8,4096]{1,0:T(8,128)}) %all-reduce.6.cloned.1.call-update) | async-done | bytes 131088 | tf_op jit(solution)/shard_map/psum | solution.py:57
  413.9 0.8 fusion.31
  414.7 35.9 %all-gather.1 = bf16[128,32,8]{1,2,0:T(8,128)(2,1)S(1)} all-gather(bf16[1,32,8]{1,2,0:T(8,128)(2,1)S(1)} %fusion.31), channel_id=1, replica_groups=mesh['leaf'=4,'rows'=32] {'leaf','rows'}, dimensions={0}, use_global_device_ids=true | all-gather | bytes 66048 | tf_op jit(solution)/shard_map/all_gather | solution.py:81
  450.6 0.3 reshape.143
  450.9 3.1 fusion.13
  454.1 43.7 %all-gather.4.cloned.1.call-done = f32[256,4096]{1,0:T(8,128)} async-done(((f32[8,4096]{1,0:T(8,128)}), f32[256,4096]{1,0:T(8,128)}) %all-gather.4.cloned.1.call-update) | async-done | bytes 4194320 | tf_op jit(solution)/shard_map/all_gather | solution.py:86
  497.8 2.4 bitcast_reduce_fusion
  500.3 1.3 copy.71
  501.6 2.0 gather_fusion
  503.6 1.0 fusion.14
  504.7 71.7 %reduce-scatter.9.cloned.1.call-done = f32[8,128]{1,0:T(8,128)} async-done(((f32[8,4096]{1,0:T(8,128)}), f32[8,128]{1,0:T(8,128)}) %reduce-scatter.9.cloned.1.call-update) | async-done | bytes 4112 | tf_op jit(solution)/shard_map/reduce_scatter | solution.py:92
  576.3 1.6 fusion.17
  578.0 73.8 %reduce-scatter.11.cloned.1.call-done = f32[8,128]{1,0:T(8,128)} async-done(((f32[8,4096]{1,0:T(8,128)}), f32[8,128]{1,0:T(8,128)}) %reduce-scatter.11.cloned.1.call-update) | async-done | bytes 4112 | tf_op jit(solution)/shard_map/reduce_scatter | solution.py:95
  651.8 0.7 convert_element_type.38
  652.5 23.6 %all_gather.31 = bf16[8,4096]{1,0:T(8,128)(2,1)S(1)} all-gather(bf16[8,128]{1,0:T(8,128)(2,1)S(1)} %convert_element_type.38), channel_id=1, replica_groups=mesh['leaf'=4,'rows'=32] {'rows'}, dimensions={1}, use_global_device_ids=true | all-gather | bytes 67584 | tf_op jit(solution)/shard_map/all_gather | solution.py:96
  676.0 1.0 copy.72
  677.0 4.3 gather_fusion.1
  681.3 1.0 copy.73
  682.4 2.8 convolution_bitcast_fusion.1
  685.2 3.1 copy.76
  688.3 4.5 reshape.144
  692.9 76.7 %reduce-scatter.13.cloned.1.call-done = f32[64,32]{1,0:T(8,128)} async-done(((f32[2048,32]{1,0:T(8,128)}), f32[64,32]{1,0:T(8,128)}) %reduce-scatter.13.cloned.1.call-update) | async-done | bytes 8208
  769.6 0.9 reshape.145
  770.6 0.3 convolution_bitcast_fusion
  770.8 3.1 copy.78
  773.9 4.5 reshape.146
  778.5 0.7 constant_dynamic-slice_fusion
  779.1 76.7 %reduce-scatter.15.cloned.1.call-done = f32[64,32]{1,0:T(8,128)} async-done(((f32[2048,32]{1,0:T(8,128)}), f32[64,32]{1,0:T(8,128)}) %reduce-scatter.15.cloned.1.call-update) | async-done | bytes 8208
  855.8 0.9 reshape.147
  856.7 0.7 copy.74
  (49 shorter events, 1.3 us)
Async XLA Ops:
  7.2 29.2 %copy-start = (bf16[4,64,2048]{2,1,0:T(8,128)(2,1)S(1)}, bf16[4,64,2048]{2,1,0:T(8,128)(2,1)}, u32[]{:S(2)}) copy-start(bf16[4,64,2048]{2,1,0:T(8,128)(2,1)} %param.15) | copy-start | bytes 3145732
  7.2 172.4 %all-reduce.4.cloned.1.call-start = ((), (), s32[]{:S(2)}) async-start(), calls=%async_computation.4 | async-start | bytes 524288 | tf_op jit(solution)/shard_map/psum | solution.py:55
  36.3 26.3 %copy-start.7 = (s32[4]{0:T(128)S(1)}, s32[4]{0:T(128)}, u32[]{:S(2)}) copy-start(s32[4]{0:T(128)} %param.18) | copy-start | bytes 52
  74.5 3.6 copy-start.8
  74.5 106.7 %copy-start.5 = (f32[8,1,128]{2,1,0:T(1,128)S(1)}, f32[8,1,128]{2,1,0:T(1,128)}, u32[]{:S(2)}) copy-start(f32[8,1,128]{2,1,0:T(1,128)} %param.13) | copy-start | bytes 12292
  74.5 131.4 %copy-start.3 = (bf16[1,128,4096]{2,1,0:T(8,128)(2,1)S(1)}, bf16[1,128,4096]{2,1,0:T(8,128)(2,1)}, u32[]{:S(2)}) copy-start(bf16[1,128,4096]{2,1,0:T(8,128)(2,1)} %param.19) | copy-start | bytes 3145732
  78.0 149.7 %copy-start.1 = (bf16[1,128,4096]{2,1,0:T(8,128)(2,1)S(1)}, bf16[1,128,4096]{2,1,0:T(8,128)(2,1)}, u32[]{:S(2)}) copy-start(bf16[1,128,4096]{2,1,0:T(8,128)(2,1)} %param.20) | copy-start | bytes 3145732
  78.1 294.8 %all-reduce.8.cloned.1.call-start = ((), (), s32[]{:S(2)}) async-start(), calls=%async_computation.6 | async-start | bytes 262144 | tf_op jit(solution)/shard_map/psum | solution.py:76
  228.2 185.7 %copy-start.6 = (f32[8,32]{1,0:T(8,128)S(1)}, f32[8,32]{1,0:T(8,128)}, u32[]{:S(2)}) copy-start(f32[8,32]{1,0:T(8,128)} %param.14) | copy-start | bytes 3076
  231.0 182.9 %all-reduce.6.cloned.1.call-start = ((), (), s32[]{:S(2)}) async-start(), calls=%async_computation.5 | async-start | bytes 262144 | tf_op jit(solution)/shard_map/psum | solution.py:57
  231.8 266.1 %all-gather.4.cloned.1.call-start = ((), (), s32[]{:S(2)}) async-start(), calls=%async_computation.9 | async-start | bytes 4325376 | tf_op jit(solution)/shard_map/all_gather | solution.py:86
  454.0 122.3 %reduce-scatter.9.cloned.1.call-start = ((), (), s32[]{:S(2)}) async-start(), calls=%async_computation.7 | async-start | bytes 135168 | tf_op jit(solution)/shard_map/reduce_scatter | solution.py:92
  454.1 49.5 %copy-start.2 = (bf16[1,128,4096]{2,1,0:T(8,128)(2,1)S(1)}, bf16[1,128,4096]{2,1,0:T(8,128)(2,1)}, u32[]{:S(2)}) copy-start(bf16[1,128,4096]{2,1,0:T(8,128)(2,1)} %param.20) | copy-start | bytes 3145732
  500.2 76.1 %copy-start.4 = (bf16[1,128,4096]{2,1,0:T(8,128)(2,1)S(1)}, bf16[1,128,4096]{2,1,0:T(8,128)(2,1)}, u32[]{:S(2)}) copy-start(bf16[1,128,4096]{2,1,0:T(8,128)(2,1)} %param.19) | copy-start | bytes 3145732
  504.6 147.1 %reduce-scatter.11.cloned.1.call-start = ((), (), s32[]{:S(2)}) async-start(), calls=%async_computation.8 | async-start | bytes 135168 | tf_op jit(solution)/shard_map/reduce_scatter | solution.py:95
  577.9 191.6 %reduce-scatter.13.cloned.1.call-start = ((), (), s32[]{:S(2)}) async-start(), calls=%async_computation.10 | async-start | bytes 1081344
  692.9 163.0 %reduce-scatter.15.cloned.1.call-start = ((), (), s32[]{:S(2)}) async-start(), calls=%async_computation.11 | async-start | bytes 1081344
Sparse Core Ops, SparseCore 0:
  78.2 101.3 all-reduce.3
  231.2 141.6 all-reduce.7
  375.1 38.7 all-reduce.5
  454.1 43.6 all-gather.3
  504.8 71.5 reduce-scatter.8
  580.2 71.5 reduce-scatter.10
  693.0 76.5 reduce-scatter.12
  778.6 77.1 reduce-scatter.14
